TPU v7x, 256 devices: a whole 4x4x8 slice. The times are simulated.
256 devices in a mesh: req: 4 (over y), blk: 16 (over z, x_lo), tp: 4 (over x_hi, core).
Axes of the slice: x: 4 (x_hi: 2, x_lo: 2; x = x_hi * 2 + x_lo), y: 4, z: 8, core: 2. Of those that a mesh axis runs over, the one named last changes fastest.
Arguments:
- tokens: bfloat16 [4, 2048, 5120], P('req', 'blk', 'tp'), may hold values from -6 to 6
- gain: bfloat16 [5120], replicated, may hold values from 0.5 to 1.5
- w_query: bfloat16 [5120, 5120], P('req', 'tp'), may hold values from -0.078125 to 0.078125
- b_query: bfloat16 [5120], P('tp'), may hold values from -4 to 4
- w_keyval: bfloat16 [5120, 2, 1024], P('req', None, 'tp'), may hold values from -0.078125 to 0.078125
- b_keyval: bfloat16 [2, 1024], P(None, 'tp'), may hold values from -3 to 3
- kv_cache: bfloat16 [4, 2, 112, 128, 1024], P('req', None, 'blk', None, 'tp'), may hold values from -400 to 400
- cached_pages: int32 [4], P('req'), may hold values from 1 to 64, as said below
- page_table: int32 [4, 80], P('req'), may hold values from -1 to 111, as said below
Outputs:
- attended: bfloat16 [4, 2048, 5120], P('req', 'blk', 'tp')
- new_cache: bfloat16 [4, 2, 112, 128, 1024], P('req', None, 'blk', None, 'tp')
Inputs may be any that keep to these rules, and one draw needn't show every extreme that they name: `cached_pages`: one request has the most, 64. `page_table`: entry p of a request's row is the slot (owner index of blk times 7 plus slot) of its logical page p for p below its cached pages plus 16, and -1 beyond; the live pages of a request use distinct slots; one index of blk holds at most 4 cached pages of a request; the request with 64 cached pages has exactly 4 on every index of blk.
All inputs are finite; a program needn't handle non-finite values.
Results may differ from a plain program's by a relative error of at most 0.012.
The roundings to bfloat16 on the way count: a program that leaves them out, or rounds other values in their place, can miss the bound.
Values may be sent and summed in bfloat16 or wider, within the bound.
A program may use at most 128 MiB of HBM per device.

v0:
```python
import jax
import jax.numpy as jnp
from jax import lax
from jax.sharding import PartitionSpec as P

HEAD_SIZE = 128
PAGE_TOKENS = 128


epsilon = 1e-06
rope_base = 1000000.0


def normalize(inputs, gain):
    floats = inputs.astype(jnp.float32)
    scaling = lax.rsqrt(jnp.mean(floats * floats, axis=-1, keepdims=True) + epsilon)
    return (floats * scaling * gain.astype(jnp.float32)).astype(jnp.bfloat16)


def apply_rotation(vectors, token_positions):
    halfway = vectors.shape[-1] // 2
    frequency = rope_base ** (-(jnp.arange(halfway, dtype=jnp.float32) * 2.0 / vectors.shape[-1]))
    angles = token_positions[:, None] * frequency[None, :]
    cosine = jnp.cos(angles)[:, None, :]
    sine_part = jnp.sin(angles)[:, None, :]
    leading = vectors[..., :halfway]
    trailing = vectors[..., halfway:]
    return jnp.concatenate(
        [leading * cosine - trailing * sine_part, trailing * cosine + leading * sine_part], axis=-1
    )


def attend(running, query_rows_all, key_rows, value_rows, allowed):
    scaling = HEAD_SIZE ** (-0.5)
    scores = (
        jnp.einsum("rgjd,kgd->rgjk", query_rows_all, key_rows, preferred_element_type=jnp.float32)
        * scaling
    )
    scores = jnp.where(allowed[:, None, None, :], scores, -jnp.inf)
    maxima, totals, blended = running
    fresh_max = jnp.maximum(maxima, jnp.max(scores, axis=-1))
    weights = jnp.exp(scores - fresh_max[..., None])
    decays = jnp.exp(maxima - fresh_max)
    totals = totals * decays + jnp.sum(weights, axis=-1)
    blended = blended * decays[..., None] + jnp.einsum(
        "rgjk,kgd->rgjd",
        weights.astype(jnp.bfloat16),
        value_rows,
        preferred_element_type=jnp.float32,
    )
    return (fresh_max, totals, blended)


def make_fold(usable_all, query_rows_all, kv_heads_local, running, pieces):
    count = pieces.shape[1]
    stride = max((divisor for divisor in (4, 3, 2, 1) if count % divisor == 0))

    def advance(counter, carried):
        segment = lax.dynamic_slice_in_dim(pieces, counter * stride, stride, 1)
        usable = lax.dynamic_slice_in_dim(usable_all, counter * stride, stride)
        key_rows = segment[0].reshape(stride * PAGE_TOKENS, kv_heads_local, HEAD_SIZE)
        value_rows = segment[1].reshape(stride * PAGE_TOKENS, kv_heads_local, HEAD_SIZE)
        allowed = jnp.repeat(usable, PAGE_TOKENS)[None, :]
        return attend(carried, query_rows_all, key_rows, value_rows, allowed)

    return lax.fori_loop(0, count // stride, advance, running)


def body(tokens, gain, w_query, b_query, w_keyval, b_keyval, kv_cache, cached_pages, page_table):
    whole = lax.all_gather(tokens[0], "tp", axis=1, tiled=True)
    normed = normalize(whole, gain)
    rows_here = normed.shape[0]
    query_width = w_query.shape[1]
    kv_width = w_keyval.shape[2]
    pair_width = 2 * kv_width
    pieces = (
        lax.all_gather(w_query, "req", axis=0, tiled=True),
        lax.all_gather(w_keyval, "req", axis=0, tiled=True),
    )
    count = pieces[0].shape[0]
    query_sum = jnp.dot(normed, pieces[0], preferred_element_type=jnp.float32)
    pair_sum = jnp.dot(
        normed, pieces[1].reshape(count, pair_width), preferred_element_type=jnp.float32
    )
    length = cached_pages[0]
    page_map = page_table[0]
    own_index = lax.axis_index("blk")
    cycle_size = lax.axis_size("blk")
    heads_local = query_width // HEAD_SIZE
    kv_heads_local = kv_width // HEAD_SIZE
    queries_per_group = heads_local // kv_heads_local
    token_index = own_index * rows_here + jnp.arange(rows_here, dtype=jnp.int32)
    token_positions = (length * PAGE_TOKENS + token_index).astype(jnp.float32)
    query_full = query_sum + b_query.astype(jnp.float32)
    query_rows_all = apply_rotation(
        query_full.reshape(rows_here, heads_local, HEAD_SIZE), token_positions
    ).astype(jnp.bfloat16)
    query_rows_all = query_rows_all.reshape(rows_here, kv_heads_local, queries_per_group, HEAD_SIZE)
    pair_full = pair_sum + b_keyval.reshape(pair_width).astype(jnp.float32)
    fresh_key = apply_rotation(
        pair_full[:, :kv_width].reshape(rows_here, kv_heads_local, HEAD_SIZE), token_positions
    ).astype(jnp.bfloat16)
    fresh_value = pair_full[:, kv_width:].astype(jnp.bfloat16)
    fresh_pages = jnp.stack([fresh_key.reshape(rows_here, kv_width), fresh_value]).reshape(
        2, rows_here // PAGE_TOKENS, PAGE_TOKENS, kv_width
    )
    every_page = lax.all_gather(fresh_pages, "blk", axis=1, tiled=True)
    new_count = every_page.shape[1]
    fresh_rows = new_count * PAGE_TOKENS
    new_keys = every_page[0].reshape(fresh_rows, kv_heads_local, HEAD_SIZE)
    new_values = every_page[1].reshape(fresh_rows, kv_heads_local, HEAD_SIZE)
    allowed_fresh = jnp.arange(fresh_rows, dtype=jnp.int32)[None, :] <= token_index[:, None]
    starting = (
        jnp.full((rows_here, kv_heads_local, queries_per_group), -jnp.inf, jnp.float32),
        jnp.zeros((rows_here, kv_heads_local, queries_per_group), jnp.float32),
        jnp.zeros((rows_here, kv_heads_local, queries_per_group, HEAD_SIZE), jnp.float32),
    )
    running = attend(starting, query_rows_all, new_keys, new_values, allowed_fresh)
    cache_storage = kv_cache[0]
    slot_count = cache_storage.shape[1]
    new_slots = lax.dynamic_slice_in_dim(page_map, length, new_count)
    chooser = (
        new_slots[None, :]
        == own_index * slot_count + jnp.arange(slot_count, dtype=jnp.int32)[:, None]
    )
    written = jnp.einsum(
        "sj,cjpw->cspw",
        chooser.astype(jnp.bfloat16),
        every_page,
        preferred_element_type=jnp.float32,
    ).astype(jnp.bfloat16)
    landed = jnp.any(chooser, axis=1)
    new_storage = jnp.where(landed[None, :, None, None], written, cache_storage)
    pool_size = cycle_size * slot_count
    live = jnp.arange(page_map.shape[0], dtype=jnp.int32) < length
    matches = (page_map[None, :] == jnp.arange(pool_size, dtype=jnp.int32)[:, None]) & live[None, :]
    valid = jnp.any(matches, axis=1)
    running = make_fold(
        valid,
        query_rows_all,
        kv_heads_local,
        running,
        lax.all_gather(cache_storage, "blk", axis=1, tiled=True),
    )
    maxima, totals, blended = running
    result = (blended / totals[..., None]).reshape(rows_here, query_width).astype(jnp.bfloat16)
    return (result[None], new_storage[None])


def solution(mesh):
    return jax.shard_map(
        body,
        mesh=mesh,
        in_specs=(
            P("req", "blk", "tp"),
            P(),
            P("req", "tp"),
            P("tp"),
            P("req", None, "tp"),
            P(None, "tp"),
            P("req", None, "blk", None, "tp"),
            P("req"),
            P("req", None),
        ),
        out_specs=(P("req", "blk", "tp"), P("req", None, "blk", None, "tp")),
        check_vma=False,
    )
```

profile of v0, /device:TPU:224, one launch (start us, length us, event | category | flops | bytes accessed | tf_op | source)
XLA Modules:
  0.0 767.5 jit_solution(6554469855381495535)
XLA Ops:
  11.2 23.9 %all-gather.13.cloned.1.call-done = bf16[1,128,5120]{2,1,0:T(8,128)(2,1)} async-done(((bf16[1,128,1280]{2,1,0:T(8,128)(2,1)}), bf16[1,128,5120]{2,1,0:T(8,128)(2,1)}) %all-gather.13.cloned.1.call-update) | async-done | bytes 1310736 | tf_op jit(solution)/shard_map/all_gather | solution.py:70
  36.7 59.2 %all-gather.9.cloned.1.call-done = bf16[5120,2,256]{2,1,0:T(2,128)(2,1)} async-done(((bf16[1280,2,256]{2,1,0:T(2,128)(2,1)}), bf16[5120,2,256]{2,1,0:T(2,128)(2,1)}) %all-gather.9.cloned.1.call-update) | async-done | bytes 5242896 | tf_op jit(solution)/shard_map/all_gather | solution.py:78
  95.9 3.5 copy.82
  104.2 69.0 %all-gather.15.cloned.1.call-done = bf16[2,2048,256]{2,1,0:T(8,128)(2,1)} async-done(((bf16[2,128,256]{2,1,0:T(8,128)(2,1)}), bf16[2,2048,256]{2,1,0:T(8,128)(2,1)}) %all-gather.15.cloned.1.call-update) | async-done | bytes 2097168 | tf_op jit(solution)/shard_map/all_gather | solution.py:107
  176.6 3.5 fusion.40
  181.2 119.4 %all-gather.11.cloned.1.call-done = bf16[5120,1280]{1,0:T(8,128)(2,1)} async-done(((bf16[1280,1280]{1,0:T(8,128)(2,1)}), bf16[5120,1280]{1,0:T(8,128)(2,1)}) %all-gather.11.cloned.1.call-update) | async-done | bytes 13107216 | tf_op jit(solution)/shard_map/all_gather | solution.py:77
  300.7 6.6 convolution_add_fusion
  313.7 3.6 fusion.46
  317.3 294.9 %all-gather.17.cloned.1.call-done = bf16[1,2,112,128,256]{4,3,2,1,0:T(8,128)(2,1)} async-done(((bf16[1,2,7,128,256]{4,3,2,1,0:T(8,128)(2,1)}), bf16[1,2,112,128,256]{4,3,2,1,0:T(8,128)(2,1)}) %all-gather.17.cloned.1.call-update) | async-done | bytes 14680080 | tf_op jit(solution)/shard_map/all_gather | solution.py:143
  612.2 146.7 %while.17 = (s32[]{:T(128)}, f32[128,2,5]{0,2,1:T(8,128)S(1)}, f32[128,2,5]{0,2,1:T(8,128)S(1)}, f32[128,2,5,128]{0,3,2,1:T(8,128)}, pred[112]{0:T(512)(128)(4,1...) while((s32[]{:T(128)}, f32[128,2,5]{0,2,1:T(8,128)S(1)}, ...), condition=%wide.region_7.8_spmd, body=%wide.region_4.0_spmd.sunk | while | flops 343083520 | bytes 12208327 | solution.py:66
  614.7 2.7 fusion.76
  620.0 2.7 fusion.76
  625.2 2.7 fusion.76
  630.4 2.7 fusion.76
  635.7 2.7 fusion.76
  640.9 2.7 fusion.76
  646.2 2.7 fusion.76
  651.4 2.7 fusion.76
  656.6 2.7 fusion.76
  661.9 2.7 fusion.76
  667.1 2.7 fusion.76
  672.3 2.7 fusion.76
  677.6 2.7 fusion.76
  682.8 2.7 fusion.76
  688.1 2.7 fusion.76
  693.3 2.7 fusion.76
  698.5 2.7 fusion.76
  709.0 2.7 fusion.76
  719.5 2.7 fusion.76
  730.0 2.7 fusion.76
  740.4 2.7 fusion.76
  750.9 2.7 fusion.76
  (345 shorter events, 108.2 us)
Async XLA Ops:
  7.2 27.9 %all-gather.13.cloned.1.call-start = ((), (), s32[]{:S(2)}) async-start(), calls=%async_computation.2 | async-start | bytes 1638400 | tf_op jit(solution)/shard_map/all_gather | solution.py:70
  7.9 88.0 %all-gather.9.cloned.1.call-start = ((), (), s32[]{:S(2)}) async-start(), calls=%async_computation | async-start | bytes 6553600 | tf_op jit(solution)/shard_map/all_gather | solution.py:78
  8.6 164.5 %all-gather.15.cloned.1.call-start = ((), (), s32[]{:S(2)}) async-start(), calls=%async_computation.3 | async-start | bytes 2228224 | tf_op jit(solution)/shard_map/all_gather | solution.py:107
  95.9 3.5 copy-start
  100.4 2.4 copy-start.3
  100.4 2.5 copy-start.4
  101.7 199.0 %all-gather.11.cloned.1.call-start = ((), (), s32[]{:S(2)}) async-start(), calls=%async_computation.1 | async-start | bytes 16384000 | tf_op jit(solution)/shard_map/all_gather | solution.py:77
  102.3 509.9 %all-gather.17.cloned.1.call-start = ((), (), s32[]{:S(2)}) async-start(), calls=%async_computation.4 | async-start | bytes 15597568 | tf_op jit(solution)/shard_map/all_gather | solution.py:143
  307.3 2.6 copy-start.2
  307.5 2.4 copy-start.1
Sparse Core Ops, SparseCore 0:
  9.8 25.1 all-gather.12
  36.9 59.0 all-gather.8
  101.8 71.3 all-gather.14
  174.8 125.7 all-gather.10
  302.3 309.8 all-gather.16
where the time goes:
time: 776 us; the launch traced here: 767 us
  waiting for transfers between devices  569 us (73%)
  matrix products  107 us (14%)
  local copies, waits for them, and re-layouts  48.8 us (6%)
  other arithmetic  26.9 us (3%)
  between operations  14.7 us (2%)
    all_gather x1, waiting for transfers between devices, body(): lax.all_gather(cache_storage, 'blk', axis=1, tiled=True)  295 us
    all_gather x1, waiting for transfers between devices, body(): lax.all_gather(w_query, 'req', axis=0, tiled=True)  119 us
    dot_general x29, matrix products, attend(): jnp.einsum('rgjk,kgd->rgjd', weights.astype(jnp.bfloat16), value_rows, pr...  79.7 us
    all_gather x1, waiting for transfers between devices, body(): every_page = lax.all_gather(fresh_pages, 'blk', axis=1, tiled=True)  69 us
    all_gather x1, waiting for transfers between devices, body(): lax.all_gather(w_keyval, 'req', axis=0, tiled=True)  59.2 us
    slice x28, local copies, waits for them, and re-layouts, advance(): segment[1].reshape(stride * PAGE_TOKENS, kv_heads_local, HEAD_SIZE)  29.8 us
    all_gather x1, waiting for transfers between devices, body(): whole = lax.all_gather(tokens[0], 'tp', axis=1, tiled=True)  23.9 us
    reduce_sum x29, other arithmetic, attend(): totals = totals * decays + jnp.sum(weights, axis=-1)  18.7 us
  transfers between devices with their start and end apart: 5, of which 5 were waited for; matrix products, arithmetic and copies ran while one was open for 4% of the time, Pallas kernels for 0%

commit v1 on v0

v1 whole, which is shorter than its diff:
```python
import functools

import jax
import jax.numpy as jnp
from jax import lax
from jax.experimental import pallas as pl
from jax.experimental.pallas import tpu as pltpu
from jax.sharding import PartitionSpec as P

HEAD = 128
PAGE = 128
SLOTS = 7
CPD = 4
EPS = 1e-06
ROPE_BASE = 1000000.0
LOG2E = 1.4426950408889634
NEG = -1e30
MESH = pl.DeviceIdType.MESH


def kernel(
    sel_ref, new_idx_ref, new_land_ref,
    tok_hbm, gain_ref, wq_hbm, wkv_hbm, bias_ref, cos_ref, sin_ref, mask_ref, kv_hbm,
    out_ref, cache_out,
    tok_all, nrm, xr, w_ref, part, ring, kv_own, kv_all, fr_all, q_ref, m_ref, l_ref, acc_ref,
    loc_sem, a_send, a_recv, y_send, y_recv, ys_send, ys_recv, b_send, b_recv,
    kz_send, kz_recv, kx_send, kx_recv, fz_send, fz_recv, fx_send, fx_recv,
):
    r = lax.axis_index("req")
    b = lax.axis_index("blk")
    t = lax.axis_index("tp")
    z, xl = b // 2, b % 2
    core = t % 2
    sib = t + 1 - 2 * core
    far = (t + 2) % 4
    sib_far = (sib + 2) % 4
    pair = b + 1 - 2 * xl
    chunk = tok_hbm.shape[1]
    rows = tok_hbm.shape[0]
    half = rows // 2
    started = []

    def at_z(delta):
        return ((z + delta + 8) % 8) * 2 + xl

    def copy(src, dst, send, recv, **device):
        return pltpu.make_async_remote_copy(
            src_ref=src, dst_ref=dst, send_sem=send, recv_sem=recv,
            device_id=device, device_id_type=MESH,
        )

    def send(src, dst, send_sem, recv_sem, **device):
        c = copy(src, dst, send_sem, recv_sem, **device)
        c.start()
        started.append(c)

    def await_recv(dst, send_sem, recv_sem, **device):
        copy(dst, dst, send_sem, recv_sem, **device).wait_recv()

    tok_in = pltpu.make_async_copy(tok_hbm, tok_all.at[t], loc_sem.at[0])
    tok_in.start()
    kv_in = pltpu.make_async_copy(kv_hbm, kv_own, loc_sem.at[1])
    kv_in.start()
    w_in = [
        pltpu.make_async_copy(wkv_hbm.at[:, 0:256], w_ref.at[:, 0:256], loc_sem.at[2]),
        pltpu.make_async_copy(wq_hbm.at[:, 0:640], w_ref.at[:, 256:896], loc_sem.at[3]),
        pltpu.make_async_copy(wkv_hbm.at[:, 256:512], w_ref.at[:, 896:1152], loc_sem.at[4]),
        pltpu.make_async_copy(wq_hbm.at[:, 640:1280], w_ref.at[:, 1152:1792], loc_sem.at[5]),
    ]
    for c in w_in:
        c.start()

    barrier = pltpu.get_barrier_semaphore()
    peers = [dict(tp=sib), dict(tp=far), dict(blk=pair), dict(blk=at_z(1)), dict(blk=at_z(-1))]
    peers += [dict(req=(r + d) % 4) for d in (1, 2, 3)]
    for peer in peers:
        pl.semaphore_signal(barrier, inc=1, device_id=peer, device_id_type=MESH)
    pl.semaphore_wait(barrier, len(peers))

    tok_in.wait()
    send(tok_all.at[t], tok_all.at[t], a_send.at[1], a_recv.at[1], tp=far)
    send(tok_all.at[t], tok_all.at[t], a_send.at[0], a_recv.at[0], tp=sib)

    kv_in.wait()
    for j in range(CPD):
        s = sel_ref[j]
        for c in range(2):
            kv_all[b, c, j * PAGE:(j + 1) * PAGE, :] = kv_own[c, s]

    def kz_region(direction, step, piece, origin):
        block = origin * 2 + (xl if piece == 0 else 1 - xl)
        size = 512 if piece == 0 else 256
        lo, n = 0, size
        if step == 3:
            n = size // 2
            lo = 0 if direction == 0 else n
        return kv_all.at[block, :, lo:lo + n, :]

    def kz_send_piece(direction, step, piece):
        sign = 1 if direction == 0 else -1
        origin = (z - sign * step + 8) % 8
        region = kz_region(direction, step, piece, origin)
        send(region, region, kz_send.at[direction, step, piece], kz_recv.at[direction, step, piece],
             blk=at_z(sign))

    def kz_await(direction, step, piece):
        sign = 1 if direction == 0 else -1
        origin = (z - sign * (step + 1) + 8) % 8
        region = kz_region(direction, step, piece, origin)
        await_recv(region, kz_send.at[direction, step, piece], kz_recv.at[direction, step, piece],
                   blk=at_z(sign))
        return origin

    def kx_send_tail(origin, k):
        region = kv_all.at[origin * 2 + xl, :, 256:512, :]
        send(region, region, kx_send.at[k], kx_recv.at[k], blk=pair)

    def kx_await_tail(origin, k):
        region = kv_all.at[origin * 2 + 1 - xl, :, 256:512, :]
        await_recv(region, kx_send.at[k], kx_recv.at[k], blk=pair)

    tails = []

    def kv_advance(step):
        for piece in range(2):
            for direction in range(2):
                origin = kz_await(direction, step, piece)
                if step < 3:
                    kz_send_piece(direction, step + 1, piece)
                if piece == 0 and (step < 3 or direction == 1):
                    tails.append(origin)
                    kx_send_tail(origin, len(tails))

    for direction in range(2):
        kz_send_piece(direction, 0, 0)

    await_recv(tok_all.at[far], a_send.at[1], a_recv.at[1], tp=far)
    send(tok_all.at[far], tok_all.at[far], a_send.at[2], a_recv.at[2], tp=sib)
    head_rows = kv_all.at[b, :, 0:256, :]
    send(head_rows, head_rows, kx_send.at[8], kx_recv.at[8], blk=pair)
    kx_send_tail(z, 0)
    await_recv(tok_all.at[sib], a_send.at[0], a_recv.at[0], tp=sib)
    await_recv(tok_all.at[sib_far], a_send.at[2], a_recv.at[2], tp=sib)

    total = jnp.zeros((rows, 1), jnp.float32)
    for c in range(4):
        x = tok_all[c].astype(jnp.float32)
        total = total + jnp.sum(x * x, axis=1, keepdims=True)
    scaling = lax.rsqrt(total / (4 * chunk) + EPS)
    for c in range(4):
        x = tok_all[c].astype(jnp.float32)
        nrm[c] = (x * scaling * gain_ref[:, c * chunk:(c + 1) * chunk]).astype(jnp.bfloat16)

    def y_half(c):
        return pl.ds(c * half, half)

    for d in (2, 1, 3):
        dest = (r + d) % 4
        mine = pl.ds(pl.multiple_of(core * half, half), half)
        send(nrm.at[dest, mine], xr.at[r, mine], y_send.at[d - 1], y_recv.at[d - 1], req=dest)

    for c in w_in:
        c.wait()

    tiles = w_ref.shape[1] // 256

    def project(slot, lhs_of):
        def tile(i, carry):
            cols = pl.ds(pl.multiple_of(i * 256, 256), 256)
            part[slot, :, cols] = jnp.dot(lhs_of(), w_ref[:, cols], preferred_element_type=jnp.float32)
            return carry

        lax.fori_loop(0, tiles, tile, 0)

    project(r, lambda: nrm[r])

    await_recv(kv_all.at[pair, :, 0:256, :], kx_send.at[8], kx_recv.at[8], blk=pair)
    for direction in range(2):
        kz_send_piece(direction, 0, 1)

    mine = pl.ds(pl.multiple_of(core * half, half), half)
    other = pl.ds(pl.multiple_of((1 - core) * half, half), half)
    for d in (1, 3, 2):
        origin = (r + 4 - d) % 4
        await_recv(xr.at[origin, mine], y_send.at[d - 1], y_recv.at[d - 1], req=(r + d) % 4)
        send(xr.at[origin, mine], xr.at[origin, mine], ys_send.at[d - 1], ys_recv.at[d - 1], tp=sib)

    spans = ((0, 256), (256, 640))

    def b_send_piece(direction, step, piece):
        sign = 1 if direction == 0 else -1
        dest = (r + 4 - sign * (step + 1)) % 4
        lo = direction * 896 + spans[piece][0]
        n = spans[piece][1]
        src = part.at[dest, :, lo:lo + n]
        dst = ring.at[step, :, lo:lo + n]
        send(src, dst, b_send.at[direction, step, piece], b_recv.at[direction, step, piece],
             req=(r + 4 + sign) % 4)

    def b_take(direction, step, piece):
        sign = 1 if direction == 0 else -1
        dest = (r + 4 - sign * (step + 2)) % 4
        lo = direction * 896 + spans[piece][0]
        n = spans[piece][1]
        await_recv(ring.at[step, :, lo:lo + n], b_send.at[direction, step, piece],
                   b_recv.at[direction, step, piece], req=(r + 4 + sign) % 4)
        part[dest, :, lo:lo + n] += ring[step, :, lo:lo + n]

    for d in (1, 3, 2):
        origin = (r + 4 - d) % 4
        await_recv(xr.at[origin, other], ys_send.at[d - 1], ys_recv.at[d - 1], tp=sib)
        project(origin, lambda: xr[origin])
        if d == 1:
            for piece in range(2):
                b_send_piece(0, 0, piece)
        if d == 3:
            for piece in range(2):
                b_send_piece(1, 0, piece)

    kv_advance(0)
    for step in range(2):
        for piece in range(2):
            for direction in range(2):
                b_take(direction, step, piece)
                b_send_piece(direction, step + 1, piece)
        kv_advance(step + 1)

    def rotate(v):
        return v * cos_ref[...] + pltpu.roll(v, 64, 1) * sin_ref[...]

    def fresh_page(block):
        return fr_all.at[block]

    def fz_block(origin, piece):
        return origin * 2 + (xl if piece == 0 else 1 - xl)

    def fz_send_piece(direction, step, piece):
        sign = 1 if direction == 0 else -1
        origin = (z - sign * step + 8) % 8
        region = fresh_page(fz_block(origin, piece))
        send(region, region, fz_send.at[direction, step, piece], fz_recv.at[direction, step, piece],
             blk=at_z(sign))

    def fz_await(direction, step, piece):
        sign = 1 if direction == 0 else -1
        origin = (z - sign * (step + 1) + 8) % 8
        region = fresh_page(fz_block(origin, piece))
        await_recv(region, fz_send.at[direction, step, piece], fz_recv.at[direction, step, piece],
                   blk=at_z(sign))

    for direction in range(2):
        b_take(direction, 2, 0)
    for h in range(2):
        k = part[r, :, h * HEAD:(h + 1) * HEAD] + bias_ref[:, h * HEAD:(h + 1) * HEAD]
        fr_all[b, 0, :, h * HEAD:(h + 1) * HEAD] = rotate(k).astype(jnp.bfloat16)
    fr_all[b, 1, :, :] = (part[r, :, 896:1152] + bias_ref[:, 896:1152]).astype(jnp.bfloat16)
    send(fresh_page(b), fresh_page(b), fx_send, fx_recv, blk=pair)
    for direction in range(2):
        fz_send_piece(direction, 0, 0)
    for direction in range(2):
        b_take(direction, 2, 1)
    for h in range(2):
        for j in range(5):
            lo = h * 896 + 256 + j * HEAD
            q = part[r, :, lo:lo + HEAD] + bias_ref[:, lo:lo + HEAD]
            q_ref[h, j * rows:(j + 1) * rows, :] = rotate(q).astype(jnp.bfloat16)

    kv_advance(3)
    kx_await_tail(z, 0)
    for k, origin in enumerate(tails):
        kx_await_tail(origin, k + 1)

    m_ref[...] = jnp.full(m_ref.shape, NEG, jnp.float32)
    l_ref[...] = jnp.zeros(l_ref.shape, jnp.float32)
    acc_ref[...] = jnp.zeros(acc_ref.shape, jnp.float32)
    factor = HEAD ** (-0.5) * LOG2E

    def attend(h, k, v, adjust):
        s = lax.dot_general(q_ref[h], k, (((1,), (1,)), ((), ())), preferred_element_type=jnp.float32)
        s = adjust(s * factor)
        m_old = m_ref[h]
        m_new = jnp.maximum(m_old, jnp.max(s, axis=1, keepdims=True))
        p = jnp.exp2(s - m_new)
        decay = jnp.exp2(m_old - m_new)
        m_ref[h] = m_new
        l_ref[h] = l_ref[h] * decay + jnp.sum(p, axis=1, keepdims=True)
        acc_ref[h] = acc_ref[h] * decay + jnp.dot(
            p.astype(jnp.bfloat16), v, preferred_element_type=jnp.float32
        )

    def cached_block(i, carry):
        bias_row = mask_ref[i]
        for h in range(2):
            cols = slice(h * HEAD, (h + 1) * HEAD)
            attend(h, kv_all[i, 0, :, cols], kv_all[i, 1, :, cols], lambda s: s + bias_row)
        return carry

    def cached(lo, hi):
        lax.fori_loop(lo, hi, cached_block, 0)

    cached(0, 3)
    await_recv(fresh_page(pair), fx_send, fx_recv, blk=pair)
    for direction in range(2):
        fz_send_piece(direction, 0, 1)
    cached(3, 5)
    done = 5
    for step in range(4):
        for piece in range(2):
            for direction in range(2):
                if step == 3 and piece != direction:
                    continue
                fz_await(direction, step, piece)
                if step < 2 or (step == 2 and piece == direction):
                    fz_send_piece(direction, step + 1, piece)
            if step < 3:
                upto = min(done + 2, 16)
                cached(done, upto)
                done = upto
    if done < 16:
        cached(done, 16)

    for s in range(SLOTS):
        i = new_idx_ref[s]
        land = jnp.broadcast_to(new_land_ref[s], (PAGE, 256)) > 0
        for c in range(2):
            kv_own[c, s] = jnp.where(land, fr_all[i, c], kv_own[c, s])
    cache_copy = pltpu.make_async_copy(kv_own, cache_out, loc_sem.at[6])
    cache_copy.start()

    def fresh_pair(i, carry):
        for h in range(2):
            cols = slice(h * HEAD, (h + 1) * HEAD)
            k = jnp.concatenate([fr_all[2 * i, 0, :, cols], fr_all[2 * i + 1, 0, :, cols]], axis=0)
            v = jnp.concatenate([fr_all[2 * i, 1, :, cols], fr_all[2 * i + 1, 1, :, cols]], axis=0)
            attend(h, k, v, lambda s: s)
        return carry

    lax.fori_loop(0, z, fresh_pair, 0)
    shape = (5 * rows, 2 * PAGE)
    token = lax.broadcasted_iota(jnp.int32, shape, 0) % rows + xl * rows
    allowed = lax.broadcasted_iota(jnp.int32, shape, 1) <= token
    for h in range(2):
        cols = slice(h * HEAD, (h + 1) * HEAD)
        k = jnp.concatenate([fr_all[2 * z, 0, :, cols], fr_all[2 * z + 1, 0, :, cols]], axis=0)
        v = jnp.concatenate([fr_all[2 * z, 1, :, cols], fr_all[2 * z + 1, 1, :, cols]], axis=0)
        attend(h, k, v, lambda s: jnp.where(allowed, s, NEG))

    for h in range(2):
        for j in range(5):
            lo = (h * 5 + j) * HEAD
            span = slice(j * rows, (j + 1) * rows)
            out_ref[:, lo:lo + HEAD] = (acc_ref[h, span] / l_ref[h, span]).astype(jnp.bfloat16)

    cache_copy.wait()
    for c in started:
        c.wait_send()


def body(tokens, gain, w_query, b_query, w_keyval, b_keyval, kv_cache, cached_pages, page_table):
    rows, chunk = tokens.shape[1], tokens.shape[2]
    query_width = w_query.shape[1]
    kv_width = w_keyval.shape[2]
    n_blk = lax.axis_size("blk")
    b = lax.axis_index("blk")
    length = cached_pages[0]
    page_map = page_table[0]
    slot_ids = jnp.arange(n_blk * SLOTS, dtype=jnp.int32)
    live = jnp.arange(page_map.shape[0], dtype=jnp.int32) < length
    valid = jnp.any((page_map[None, :] == slot_ids[:, None]) & live[None, :], axis=1)
    valid = valid.reshape(n_blk, SLOTS)
    counts = jnp.sum(valid.astype(jnp.int32), axis=1)
    mask = jnp.where(
        jnp.arange(CPD * PAGE, dtype=jnp.int32)[None, :] // PAGE < counts[:, None], 0.0, NEG
    ).astype(jnp.float32)[:, None, :]
    own = lax.dynamic_slice_in_dim(valid, b, 1, 0)[0].astype(jnp.int32)
    slots = jnp.arange(SLOTS, dtype=jnp.int32)
    before = jnp.sum(own[None, :] * (slots[None, :] < slots[:, None]).astype(jnp.int32), axis=1)
    picks = jnp.arange(CPD, dtype=jnp.int32)
    sel = jnp.sum(
        slots[None, :] * ((before[None, :] == picks[:, None]) & (own[None, :] > 0)).astype(jnp.int32), axis=1
    )
    new_slots = lax.dynamic_slice_in_dim(page_map, length, n_blk)
    chooser = new_slots[None, :] == b * SLOTS + slots[:, None]
    new_idx = jnp.sum(jnp.arange(n_blk, dtype=jnp.int32)[None, :] * chooser.astype(jnp.int32), axis=1)
    new_land = jnp.any(chooser, axis=1).astype(jnp.int32)

    half_head = HEAD // 2
    frequency = ROPE_BASE ** (-(jnp.arange(half_head, dtype=jnp.float32) * 2.0 / HEAD))
    token_index = b * rows + jnp.arange(rows, dtype=jnp.int32)
    angles = (length * PAGE + token_index).astype(jnp.float32)[:, None] * frequency[None, :]
    cosine, sine = jnp.cos(angles), jnp.sin(angles)
    cos_full = jnp.concatenate([cosine, cosine], axis=1)
    sin_full = jnp.concatenate([-sine, sine], axis=1)

    bq = b_query.astype(jnp.float32)
    bkv = b_keyval.astype(jnp.float32)
    bias = jnp.concatenate([bkv[0], bq[:640], bkv[1], bq[640:]])[None, :]

    vmem = pl.BlockSpec(memory_space=pltpu.VMEM)
    smem = pl.BlockSpec(memory_space=pltpu.SMEM)
    hbm = pl.BlockSpec(memory_space=pl.ANY)
    bf, f32 = jnp.bfloat16, jnp.float32
    dma = pltpu.SemaphoreType.DMA
    width = query_width + 2 * kv_width
    attended, new_cache = pl.pallas_call(
        kernel,
        out_shape=(
            jax.ShapeDtypeStruct((rows, query_width), bf),
            jax.ShapeDtypeStruct(kv_cache.shape[1:], bf),
        ),
        in_specs=[smem] * 3 + [hbm, vmem, hbm, hbm, vmem, vmem, vmem, vmem, hbm],
        out_specs=(vmem, hbm),
        scratch_shapes=[
            pltpu.VMEM((4, rows, chunk), bf),
            pltpu.VMEM((4, rows, chunk), bf),
            pltpu.VMEM((4, rows, chunk), bf),
            pltpu.VMEM((chunk, width), bf),
            pltpu.VMEM((4, rows, width), f32),
            pltpu.VMEM((3, rows, width), f32),
            pltpu.VMEM(kv_cache.shape[1:], bf),
            pltpu.VMEM((n_blk, 2, CPD * PAGE, kv_width), bf),
            pltpu.VMEM((n_blk, 2, PAGE, kv_width), bf),
            pltpu.VMEM((2, 5 * rows, HEAD), bf),
            pltpu.VMEM((2, 5 * rows, 1), f32),
            pltpu.VMEM((2, 5 * rows, 1), f32),
            pltpu.VMEM((2, 5 * rows, HEAD), f32),
            dma((7,)), dma((3,)), dma((3,)), dma((3,)), dma((3,)), dma((3,)), dma((3,)),
            dma((2, 3, 2)), dma((2, 3, 2)),
            dma((2, 4, 2)), dma((2, 4, 2)), dma((9,)), dma((9,)),
            dma((2, 4, 2)), dma((2, 4, 2)), dma, dma,
        ],
        compiler_params=pltpu.CompilerParams(
            collective_id=0, has_side_effects=True, vmem_limit_bytes=60 * 1024 * 1024
        ),
    )(
        sel, new_idx, new_land,
        tokens[0], gain.astype(f32)[None, :], w_query, w_keyval.reshape(chunk, 2 * kv_width), bias,
        cos_full, sin_full, mask, kv_cache[0],
    )
    return attended[None], new_cache[None]


def solution(mesh):
    return jax.shard_map(
        body,
        mesh=mesh,
        in_specs=(
            P("req", "blk", "tp"),
            P(),
            P("req", "tp"),
            P("tp"),
            P("req", None, "tp"),
            P(None, "tp"),
            P("req", None, "blk", None, "tp"),
            P("req"),
            P("req", None),
        ),
        out_specs=(P("req", "blk", "tp"), P("req", None, "blk", None, "tp")),
        check_vma=False,
    )
```

time: 776 us -> 178 us (0.23); the launches traced: 767 us -> 177 us
  waiting for transfers between devices: 569 us -> 0 us
  Pallas kernels: 0 us -> 160 us
  matrix products: 107 us -> 0 us
  local copies, waits for them, and re-layouts: 48.8 us -> 9.48 us
  other arithmetic: 26.9 us -> 6.25 us
  between operations: 14.7 us -> 1.35 us
    all_gather x5 -> x0, waiting for transfers between devices: 566 us -> none  [the longest x1 295 us: body(): lax.all_gather(cache_storage, 'blk', axis=1, tiled=True)]
    pallas_call x0 -> x1, Pallas kernels: none -> 160 us  [body(): pl.pallas_call(kernel, out_shape=(jax.ShapeDtypeStruct((rows, query_width...]
    dot_general x61 -> x0, matrix products: 107 us -> none  [the longest x29 79.7 us: attend(): jnp.einsum('rgjk,kgd->rgjd', weights.astype(jnp.bfloat16), value_rows, pr...]
    slice x30 -> x2, local copies, waits for them, and re-layouts: 31.5 us -> 1.52 us  [body(): bias = jnp.concatenate([bkv[0], bq[:640], bkv[1], bq[640:]])[None, :]]
    reduce_sum x30 -> x4, other arithmetic: 20.4 us -> 1.63 us  [the longest x1 0.7 us: body(): jnp.sum(slots[None, :] * ((before[None, :] == picks[:, None]) & (own[None...]
  transfers between devices with their start and end apart: 5 -> 0, of which waited for: 5 -> 0; matrix products, arithmetic and copies ran while one was open for 4% -> 0% of each run, Pallas kernels for 0% -> 0%
where the time goes in v1:
time: 178 us; the launch traced here: 177 us
  Pallas kernels  160 us (90%)
  local copies, waits for them, and re-layouts  9.48 us (5%)
  other arithmetic  6.25 us (4%)
    pallas_call x1, Pallas kernels, body(): pl.pallas_call(kernel, out_shape=(jax.ShapeDtypeStruct((rows, query_width...  160 us
    unnamed x3, local copies, waits for them, and re-layouts  6.53 us

profile of v1, /device:TPU:224, one launch (start us, length us, event | category | flops | bytes accessed | tf_op | source)
XLA Modules:
  0.0 177.4 jit_solution(13536119155529539974)
XLA Ops:
  1.3 0.7 dynamic-slice_bitcast_fusion
  2.1 0.8 fusion.1
  2.8 0.2 compare_reduce_fusion
  3.0 0.7 fusion.3.new_idx_ref
  3.7 0.6 convert_element_type.29.new_land_ref
  4.3 0.1 reshape.114
  4.4 0.1 convert_reduce_fusion
  4.5 0.1 select_reduce_fusion
  4.6 0.7 select_reduce_fusion.1.sel_ref
  5.3 0.8 fusion.10
  6.1 0.8 fusion.9
  6.9 0.6 broadcast_in_dim.20.bias_ref
  7.5 1.3 broadcast_in_dim.46
  8.8 0.7 compare_select_fusion.mask_ref
  9.5 0.3 fusion.2
  9.8 0.8 pad_maximum_fusion
  10.5 2.6 %copy.11 = bf16[160,8,2,256]{3,1,2,0:T(8,128)(2,1)} copy(bf16[160,8,2,256]{3,2,1,0:T(2,128)(2,1)} %bitcast.23) | data formatting | bytes 2621440
  13.2 160.3 %shard_map.104 = (bf16[128,1280]{1,0:T(8,128)(2,1)}, bf16[2,7,128,256]{3,2,1,0:T(8,128)(2,1)}) custom-call(s32[4]{0:T(128)} %select_reduce_fusion.1.sel_ref, s32[7]{0:T(128)} %fusion.3.new_idx_ref, s32[7]{0:T(128)} %convert_element_type.29.new_land_ref, bf16[128,1280]{1,0:T(8,128)(2,1)} %bitcast.27, f32[1,5120]{1,0:T(1,128)} %bitcast.28, ...), custom_call_target="tpu_custom_call" | custom-call | tf_op jit(solution)/shard_map/pallas_call | solution.py:405
  173.5 1.7 copy.15
  175.2 2.2 %copy.16 = bf16[1,2,7,128,256]{4,3,2,1,0:T(8,128)(2,1)} copy(bf16[1,2,7,128,256]{4,3,2,1,0:T(8,128)(2,1)} %bitcast.24) | data formatting | bytes 1835008
  (7 shorter events, 0.1 us)
